TPU v7x, 32 devices: a whole 2x2x4 slice. The times are simulated.
32 devices in a mesh: str: 8 (over z, x), fac: 4 (over y, core).
Axes of the slice: x: 2, y: 2, z: 4, core: 2. Of those that a mesh axis runs over, the one named last changes fastest.
Arguments:
- amplitudes: bfloat16 [2, 4096, 4096], P(None, 'str'), may hold values from -6 to 6
- beta_index: int32 [2, 32, 12], replicated, may hold values from 0 to 31, all different within a row; in each aligned block of 32 rows (0 to 31, 32 to 63, ..., all dimensions but the last counted through in order) at most 24 rows name the same one
- beta_tile: int32 [2, 12], replicated, may hold values from 0 to 15
- beta_flip: int32 [2, 4096], replicated, may hold values 0 or 1
- alpha_index: int32 [2, 32, 12], replicated, may hold values from 0 to 31, all different within a row; in each aligned block of 32 rows (0 to 31, 32 to 63, ..., all dimensions but the last counted through in order) at most 24 rows name the same one
- alpha_tile: int32 [2, 12], replicated, may hold values from 0 to 15
- alpha_flip: int32 [2, 4096], replicated, may hold values 0 or 1
- beta_tiles: bfloat16 [16, 128, 128], replicated, may hold values from -0.15625 to 0.15625
- alpha_tiles: bfloat16 [16, 128, 128], replicated, may hold values from -0.109375 to 0.109375
Outputs:
- sigma: float32 [2, 4096, 4096], P(None, 'fac', 'str')
Inputs may be any that keep to these rules, and one draw needn't show every extreme that they name: `beta_index`: each block row of one factor's beta operator names 12 different block columns; within one factor's operator no block column is named by more than 24 block rows, and in some factor one column is named by exactly 24. `alpha_index`: each block row of one factor's alpha operator names 12 different block columns; within one factor's operator no block column is named by more than 24 block rows, and in some factor one column is named by exactly 24.
All inputs are finite; a program needn't handle non-finite values.
Results may differ from a plain program's by a relative error of at most 0.012.
Values may be sent and summed in bfloat16 or wider, within the bound.
A program may use at most 128 MiB of HBM per device.

v0:
```python
import jax
import jax.numpy as jnp
from jax import lax
from jax.sharding import PartitionSpec as P


def apply_beta(amplitudes, block_ids, tile_ids, flips, tile_table):
    part_count, height, column_count = amplitudes.shape
    tile_size = tile_table.shape[1]
    block_count = column_count // tile_size
    signs = (1 - 2 * flips).astype(jnp.bfloat16)
    signed = amplitudes * signs[None, None, :]
    blocks = signed.reshape(part_count, height, block_count, tile_size)
    weights = tile_table[tile_ids]
    group_size = block_count // 4
    pieces = []
    for group_id in range(4):
        lower = group_id * group_size
        chosen = block_ids[lower : lower + group_size]
        gathered = blocks[:, :, chosen]
        pieces.append(
            jnp.einsum(
                "pajkc,krc->pajr", gathered, weights, preferred_element_type=jnp.float32
            ).astype(jnp.bfloat16)
        )
    return jnp.concatenate(pieces, axis=2).reshape(part_count, height, column_count)


def apply_alpha(half, block_ids, tile_ids, flips, tile_table):
    part_count, total, column_count = half.shape
    tile_size = tile_table.shape[1]
    block_count = total // tile_size
    signs = (1 - 2 * flips).astype(jnp.bfloat16)
    signed = half * signs[None, :, None]
    blocks = signed.reshape(part_count, block_count, tile_size, column_count)
    weights = tile_table[tile_ids]
    group_size = block_count // 4
    pieces = []
    for group_id in range(4):
        lower = group_id * group_size
        chosen = block_ids[lower : lower + group_size]
        gathered = blocks[:, chosen]
        pieces.append(
            jnp.einsum(
                "pjkcn,krc->pjrn", gathered, weights, preferred_element_type=jnp.float32
            ).astype(jnp.bfloat16)
        )
    return jnp.concatenate(pieces, axis=1).reshape(part_count, total, column_count)


def local(
    amplitudes,
    beta_index,
    beta_tile,
    beta_flip,
    alpha_index,
    alpha_tile,
    alpha_flip,
    beta_tiles,
    alpha_tiles,
):
    position = lax.axis_index("fac")
    factor = position // 2
    part = position % 2
    own_part = lax.dynamic_index_in_dim(amplitudes, part, 0, keepdims=True)
    beta_ids = lax.dynamic_index_in_dim(beta_index, factor, 0, keepdims=False)
    beta_kinds = lax.dynamic_index_in_dim(beta_tile, factor, 0, keepdims=False)
    beta_signs = lax.dynamic_index_in_dim(beta_flip, factor, 0, keepdims=False)
    half = apply_beta(own_part, beta_ids, beta_kinds, beta_signs, beta_tiles)
    alpha_ids = lax.dynamic_index_in_dim(alpha_index, factor, 0, keepdims=False)
    alpha_kinds = lax.dynamic_index_in_dim(alpha_tile, factor, 0, keepdims=False)
    alpha_signs = lax.dynamic_index_in_dim(alpha_flip, factor, 0, keepdims=False)
    mixed = apply_alpha(
        lax.all_to_all(half, "str", split_axis=2, concat_axis=1, tiled=True),
        alpha_ids,
        alpha_kinds,
        alpha_signs,
        alpha_tiles,
    )
    mixed = lax.optimization_barrier(mixed)
    selector = (jnp.arange(2) == part)[:, None, None]
    padded = jnp.where(selector, mixed.astype(jnp.float32), 0.0)
    return lax.psum_scatter(
        padded.astype(jnp.bfloat16), "fac", scatter_dimension=1, tiled=True
    ).astype(jnp.float32)


def solution(mesh):
    return jax.shard_map(
        local,
        mesh=mesh,
        in_specs=(P(None, "str", None), P(), P(), P(), P(), P(), P(), P(), P()),
        out_specs=P(None, "fac", "str"),
        check_vma=False,
    )
```

profile of v0, /device:TPU:0, one launch (start us, length us, event | category | flops | bytes accessed | tf_op | source)
XLA Modules:
  0.0 445.0 jit_solution(6631989853623679221)
XLA Ops:
  11.3 6.5 %copy.44 = bf16[1,512,4096]{1,2,0:T(8,128)(2,1)} copy(bf16[1,512,4096]{2,1,0:T(8,128)(2,1)} %constant_dynamic-slice_fusion.9) | data formatting | bytes 8388608
  21.9 6.4 %copy.28 = bf16[512,32,128]{2,0,1:T(8,128)(2,1)} copy(bf16[512,32,128]{0,2,1:T(8,128)(2,1)} %bitcast.181) | data formatting | bytes 8388608 | tf_op jit(solution)/shard_map/reshape | solution.py:13
  28.8 9.0 %gather_fusion.1 = bf16[96,512,128]{2,1,0:T(8,128)(2,1)} fusion(bf16[512,32,128]{2,0,1:T(8,128)(2,1)} %copy.28, s32[1024]{0:T(1024)S(1)} %pad_clamp_fusion.8), kind=kCustom, calls=%fused_computation.1 | custom fusion | bytes 25166208 | tf_op jit(solution)/shard_map/gather | solution.py:20
  37.8 9.0 %gather_fusion.3 = bf16[96,512,128]{2,1,0:T(8,128)(2,1)} fusion(bf16[512,32,128]{2,0,1:T(8,128)(2,1)} %copy.28, s32[1024]{0:T(1024)S(1)} %pad_clamp_fusion.6), kind=kCustom, calls=%fused_computation.3 | custom fusion | bytes 25166208 | tf_op jit(solution)/shard_map/gather | solution.py:20
  47.4 8.9 %fusion = bf16[1,512,8,128]{1,3,2,0:T(8,128)(2,1)S(1)} fusion(bf16[512,8,12,128]{3,0,2,1:T(8,128)(2,1)} %bitcast.174, bf16[12,128,128]{2,1,0:T(8,128)(2,1)S(1)} %gather_fusion.2), kind=kOutput, calls=%fused_computation.24 | convolution fusion | flops 1611137024 | bytes 14024704 | tf_op jit(solution)/shard_map/pajkc,krc->pajr/dot_general | solution.py:22
  60.8 9.0 %gather_fusion.4 = bf16[96,512,128]{2,1,0:T(8,128)(2,1)} fusion(bf16[512,32,128]{2,0,1:T(8,128)(2,1)} %copy.28, s32[1024]{0:T(1024)S(1)} %pad_clamp_fusion.5), kind=kCustom, calls=%fused_computation.4 | custom fusion | bytes 25166208 | tf_op jit(solution)/shard_map/gather | solution.py:20
  69.8 9.7 %fusion.2 = bf16[1,512,8,128]{1,3,2,0:T(8,128)(2,1)} fusion(bf16[512,8,12,128]{3,0,2,1:T(8,128)(2,1)} %bitcast.177, bf16[12,128,128]{2,1,0:T(8,128)(2,1)S(1)} %gather_fusion.2), kind=kOutput, calls=%fused_computation.26 | convolution fusion | flops 1611137024 | bytes 14024704 | tf_op jit(solution)/shard_map/pajkc,krc->pajr/dot_general | solution.py:22
  79.6 9.0 %gather_fusion.5 = bf16[96,512,128]{2,1,0:T(8,128)(2,1)} fusion(bf16[512,32,128]{2,0,1:T(8,128)(2,1)} %copy.28, s32[1024]{0:T(1024)S(1)} %pad_clamp_fusion.4), kind=kCustom, calls=%fused_computation.5 | custom fusion | bytes 25166208 | tf_op jit(solution)/shard_map/gather | solution.py:20
  88.6 8.8 %fusion.3 = bf16[1,512,8,128]{1,3,2,0:T(8,128)(2,1)S(1)} fusion(bf16[512,8,12,128]{3,0,2,1:T(8,128)(2,1)} %bitcast.176, bf16[12,128,128]{2,1,0:T(8,128)(2,1)S(1)} %gather_fusion.2), kind=kOutput, calls=%fused_computation.27 | convolution fusion | flops 1611137024 | bytes 14024704 | tf_op jit(solution)/shard_map/pajkc,krc->pajr/dot_general | solution.py:22
  98.0 36.5 %copy.56 = bf16[1,512,4096]{1,0,2:T(2,128)(2,1)} copy(bf16[1,512,4096]{1,2,0:T(8,128)(2,1)S(1)} %bitcast.178) | data formatting | bytes 8388608 | tf_op jit(solution)/shard_map/reshape | solution.py:26
  135.0 28.5 %reduce.4 = bf16[4096,512]{1,0:T(8,128)(2,1)} reduce(bf16[4096,1,512]{2,1,0:T(2,128)(2,1)} %bitcast.172, bf16[]{:T(256)} %broadcast.272), dimensions={1}, to_apply=%bitcast.167.reduce_sub_computation | reduce | bytes 8388610
  163.5 7.9 %reshape.535 = bf16[8,2,131072]{2,1,0:T(2,128)(2,1)} reshape(bf16[4096,512]{1,0:T(8,128)(2,1)} %reduce.4) | data formatting | bytes 8388608
  171.4 7.3 %all-to-all-start = ((bf16[8,2,131072]{2,1,0:T(2,128)(2,1)}), bf16[8,2,131072]{2,1,0:T(2,128)(2,1)}, u32[]{:S(2)}, u32[]{:S(2)}) async-start(bf16[8,2,131072]{2,1,0:T(2,128)(2,1)} %reshape.535), calls=%async_computation | async-start | bytes 8388608 | tf_op jit(solution)/shard_map/all_to_all | solution.py:74
  180.2 91.7 %all-to-all-done = bf16[8,2,131072]{2,1,0:T(2,128)(2,1)} async-done(((bf16[8,2,131072]{2,1,0:T(2,128)(2,1)}), bf16[8,2,131072]{2,1,0:T(2,128)(2,1)}, u32[]{:S(2)}, u32[]{:S(2)}) %all-to-all-start) | async-done | bytes 4194336 | tf_op jit(solution)/shard_map/all_to_all | solution.py:74
  271.9 8.8 %reshape.536 = bf16[4096,1,512]{2,1,0:T(2,128)(2,1)} reshape(bf16[8,2,131072]{2,1,0:T(2,128)(2,1)} %all-to-all-done) | data formatting | bytes 8388608
  280.7 6.6 %copy.43 = bf16[1,512,4096]{1,2,0:T(8,128)(2,1)} copy(bf16[1,512,4096]{1,0,2:T(2,128)(2,1)} %bitcast.173) | data formatting | bytes 8388608
  287.3 6.5 %copy.33 = bf16[1,8,512,512]{3,2,1,0:T(8,128)(2,1)} copy(bf16[1,8,512,512]{2,3,1,0:T(8,128)(2,1)} %bitcast.179) | data formatting | bytes 8388608 | tf_op jit(solution)/shard_map/all_to_all | solution.py:74
  297.7 9.0 %gather_fusion.6 = bf16[96,128,512]{2,1,0:T(8,128)(2,1)} fusion(bf16[32,128,512]{2,1,0:T(8,128)(2,1)} %multiply_bitcast_fusion, s32[1024]{0:T(1024)S(1)} %pad_clamp_fusion.3), kind=kCustom, calls=%fused_computation.6 | custom fusion | bytes 25166208 | tf_op jit(solution)/shard_map/gather | solution.py:42
  306.7 9.0 %gather_fusion.7 = bf16[96,128,512]{2,1,0:T(8,128)(2,1)} fusion(bf16[32,128,512]{2,1,0:T(8,128)(2,1)} %multiply_bitcast_fusion, s32[1024]{0:T(1024)S(1)} %pad_clamp_fusion.2), kind=kCustom, calls=%fused_computation.7 | custom fusion | bytes 25166208 | tf_op jit(solution)/shard_map/gather | solution.py:42
  315.7 5.9 %fusion.4 = bf16[1,8,128,512]{3,2,1,0:T(8,128)(2,1)S(1)} fusion(bf16[8,12,128,512]{3,2,1,0:T(8,128)(2,1)} %bitcast.168, bf16[12,128,128]{2,1,0:T(8,128)(2,1)S(1)} %gather_fusion), kind=kOutput, calls=%fused_computation.28 | convolution fusion | flops 1611137024 | bytes 14024704 | tf_op jit(solution)/shard_map/pjkcn,krc->pjrn/dot_general | solution.py:44
  326.8 9.0 %gather_fusion.8 = bf16[96,128,512]{2,1,0:T(8,128)(2,1)} fusion(bf16[32,128,512]{2,1,0:T(8,128)(2,1)} %multiply_bitcast_fusion, s32[1024]{0:T(1024)S(1)} %pad_clamp_fusion.1), kind=kCustom, calls=%fused_computation.8 | custom fusion | bytes 25166208 | tf_op jit(solution)/shard_map/gather | solution.py:42
  335.9 6.7 %fusion.6 = bf16[1,8,128,512]{3,2,1,0:T(8,128)(2,1)} fusion(bf16[8,12,128,512]{3,2,1,0:T(8,128)(2,1)} %bitcast.171, bf16[12,128,128]{2,1,0:T(8,128)(2,1)S(1)} %gather_fusion), kind=kOutput, calls=%fused_computation.30 | convolution fusion | flops 1611137024 | bytes 14024704 | tf_op jit(solution)/shard_map/pjkcn,krc->pjrn/dot_general | solution.py:44
  342.5 9.0 %gather_fusion.9 = bf16[96,128,512]{2,1,0:T(8,128)(2,1)} fusion(bf16[32,128,512]{2,1,0:T(8,128)(2,1)} %multiply_bitcast_fusion, s32[1024]{0:T(1024)S(1)} %pad_clamp_fusion), kind=kCustom, calls=%fused_computation.9 | custom fusion | bytes 25166208 | tf_op jit(solution)/shard_map/gather | solution.py:42
  363.1 70.8 %reduce-scatter.2.cloned.1.call-done = bf16[2,1024,512]{2,1,0:T(8,128)(2,1)} async-done(((bf16[2,4096,512]{2,1,0:T(8,128)(2,1)}), bf16[2,1024,512]{2,1,0:T(8,128)(2,1)}) %reduce-scatter.2.cloned.1.call-update) | async-done | bytes 2097168 | tf_op jit(solution)/shard_map/reduce_scatter | solution.py:83
  (78 shorter events, 42.0 us)
Async XLA Ops:
  6.5 40.3 %copy-start = (bf16[16,128,128]{2,1,0:T(8,128)(2,1)S(1)}, bf16[16,128,128]{2,1,0:T(8,128)(2,1)}, u32[]{:S(2)}) copy-start(bf16[16,128,128]{2,1,0:T(8,128)(2,1)} %param.16) | copy-start | bytes 1572868
  6.5 11.2 %copy-start.10 = (s32[2,4096]{1,0:T(2,128)S(1)}, s32[2,4096]{1,0:T(2,128)}, u32[]{:S(2)}) copy-start(s32[2,4096]{1,0:T(2,128)} %param.15) | copy-start | bytes 98308
  6.5 11.2 %copy-start.11 = (s32[2,4096]{1,0:T(2,128)S(1)}, s32[2,4096]{1,0:T(2,128)}, u32[]{:S(2)}) copy-start(s32[2,4096]{1,0:T(2,128)} %param.12) | copy-start | bytes 98308
  17.9 10.4 %copy-start.8 = (s32[2,32,12]{1,0,2:T(2,128)S(1)}, s32[2,32,12]{1,0,2:T(2,128)}, u32[]{:S(2)}) copy-start(s32[2,32,12]{1,0,2:T(2,128)} %param.10) | copy-start | bytes 9220
  17.9 10.8 %copy-start.12 = (s32[2,12]{1,0:T(2,128)S(1)}, s32[2,12]{1,0:T(2,128)}, u32[]{:S(2)}) copy-start(s32[2,12]{1,0:T(2,128)} %param.14) | copy-start | bytes 292
  17.9 10.8 %copy-start.13 = (s32[2,12]{1,0:T(2,128)S(1)}, s32[2,12]{1,0:T(2,128)}, u32[]{:S(2)}) copy-start(s32[2,12]{1,0:T(2,128)} %param.11) | copy-start | bytes 292
  47.4 8.9 %copy-start.3 = (bf16[96,512,128]{2,1,0:T(8,128)(2,1)S(1)}, bf16[96,512,128]{2,1,0:T(8,128)(2,1)}, u32[]{:S(2)}) copy-start(bf16[96,512,128]{2,1,0:T(8,128)(2,1)} %gather_fusion.3) | copy-start | bytes 37748740
  88.6 8.8 %copy-start.6 = (bf16[1,512,8,128]{1,3,2,0:T(8,128)(2,1)S(1)}, bf16[1,512,8,128]{1,3,2,0:T(8,128)(2,1)}, u32[]{:S(2)}) copy-start(bf16[1,512,8,128]{1,3,2,0:T(8,128)(2,1)} %fusion.2) | copy-start | bytes 3145732
  163.5 15.2 %copy-start.9 = (s32[2,32,12]{1,0,2:T(2,128)S(1)}, s32[2,32,12]{1,0,2:T(2,128)}, u32[]{:S(2)}) copy-start(s32[2,32,12]{1,0,2:T(2,128)} %param.13) | copy-start | bytes 9220
  163.5 16.0 %copy-start.7 = (bf16[16,128,128]{2,1,0:T(8,128)(2,1)S(1)}, bf16[16,128,128]{2,1,0:T(8,128)(2,1)}, u32[]{:S(2)}) copy-start(bf16[16,128,128]{2,1,0:T(8,128)(2,1)} %param.17) | copy-start | bytes 1572868
  171.4 100.5 %all-to-all-start = ((bf16[8,2,131072]{2,1,0:T(2,128)(2,1)}), bf16[8,2,131072]{2,1,0:T(2,128)(2,1)}, u32[]{:S(2)}, u32[]{:S(2)}) async-start(bf16[8,2,131072]{2,1,0:T(2,128)(2,1)} %reshape.535), calls=%async_computation | async-start | bytes 8388608 | tf_op jit(solution)/shard_map/all_to_all | solution.py:74
  178.6 255.3 %reduce-scatter.2.cloned.1.call-start = ((), (), s32[]{:S(2)}) async-start(), calls=%async_computation.2 | async-start | bytes 10485760 | tf_op jit(solution)/shard_map/reduce_scatter | solution.py:83
  315.7 8.2 %copy-start.2 = (bf16[96,128,512]{2,1,0:T(8,128)(2,1)S(1)}, bf16[96,128,512]{2,1,0:T(8,128)(2,1)}, u32[]{:S(2)}) copy-start(bf16[96,128,512]{2,1,0:T(8,128)(2,1)} %gather_fusion.7) | copy-start | bytes 37748740
  351.5 5.9 %copy-start.4 = (bf16[1,8,128,512]{3,2,1,0:T(8,128)(2,1)S(1)}, bf16[1,8,128,512]{3,2,1,0:T(8,128)(2,1)}, u32[]{:S(2)}) copy-start(bf16[1,8,128,512]{3,2,1,0:T(8,128)(2,1)} %fusion.5) | copy-start | bytes 3145732
  351.5 5.9 %copy-start.5 = (bf16[1,8,128,512]{3,2,1,0:T(8,128)(2,1)S(1)}, bf16[1,8,128,512]{3,2,1,0:T(8,128)(2,1)}, u32[]{:S(2)}) copy-start(bf16[1,8,128,512]{3,2,1,0:T(8,128)(2,1)} %fusion.6) | copy-start | bytes 3145732
  358.0 80.1 %copy-start.1 = (bf16[16,128,128]{2,1,0:T(8,128)(2,1)S(1)}, bf16[16,128,128]{2,1,0:T(8,128)(2,1)}, u32[]{:S(2)}) copy-start(bf16[16,128,128]{2,1,0:T(8,128)(2,1)} %param.16) | copy-start | bytes 1572868
Sparse Core Ops, SparseCore 0:
  363.3 70.6 reduce-scatter.1
where the time goes:
time: 446 us; the launch traced here: 445 us
  waiting for transfers between devices  163 us (37%)
  local copies, waits for them, and re-layouts  161 us (36%)
  matrix products  52.9 us (12%)
  other arithmetic  47.1 us (11%)
  between operations  13.7 us (3%)
  starting transfers between devices  7.29 us (2%)
    all_to_all x1, waiting for transfers between devices, local(): lax.all_to_all(half, 'str', split_axis=2, concat_axis=1, tiled=True)  91.7 us
    reduce_scatter x1, waiting for transfers between devices, local(): lax.psum_scatter(padded.astype(jnp.bfloat16), 'fac', scatter_dimension=1,...  70.8 us
    reshape x1, local copies, waits for them, and re-layouts, apply_beta(): jnp.concatenate(pieces, axis=2).reshape(part_count, height, column_count)  36.5 us
    gather x4, local copies, waits for them, and re-layouts, apply_beta(): gathered = blocks[:, :, chosen]  36 us
    gather x4, local copies, waits for them, and re-layouts, apply_alpha(): gathered = blocks[:, chosen]  36 us
    unnamed x41, local copies, waits for them, and re-layouts  33.3 us
    dot_general x4, matrix products, apply_beta(): jnp.einsum('pajkc,krc->pajr', gathered, weights, preferred_element_type=j...  31.6 us
    unnamed x1, other arithmetic  28.5 us
  transfers between devices with their start and end apart: 2, of which 2 were waited for; matrix products, arithmetic and copies ran while one was open for 0% of the time, Pallas kernels for 0%

commit v1 on v0

v1 whole, which is shorter than its diff:
```python
import functools

import jax
import jax.numpy as jnp
from jax import lax
from jax.experimental import pallas as pl
from jax.experimental.pallas import tpu as pltpu
from jax.sharding import PartitionSpec as P

MESH = pl.DeviceIdType.MESH


def kernel(dims, amp_hbm, sign_b, sign_a, bidx, btile, aidx, atile, btab, atab, out, *scratch):
    S, F, NF, C, A, T, K = dims
    amp, half_send, term_send, wb, wa = scratch[:5]
    recv = scratch[5 : 5 + C]
    a_sem, s_send, s_recv, f_send, f_recv = scratch[5 + C :]
    me = lax.axis_index("str")
    pos = lax.axis_index("fac")
    fac = pos // 2
    part = pos % 2
    rows = A * T
    per = term_send.shape[1] // F

    def load(k):
        return pltpu.make_async_copy(amp_hbm.at[part, :, pl.ds(pl.multiple_of(k * T, T), T)], amp.at[k], a_sem.at[k])

    def start_load(k, _):
        load(k).start()
        return 0

    NB = amp.shape[0]
    lax.fori_loop(0, NB, start_load, 0)

    barrier = pltpu.get_barrier_semaphore()

    def greet_str(t, _):
        pl.semaphore_signal(barrier, inc=1, device_id={"str": (me + 1 + t) % S}, device_id_type=MESH)
        return 0

    def greet_fac(t, _):
        pl.semaphore_signal(barrier, inc=1, device_id={"fac": (pos + 1 + t) % F}, device_id_type=MESH)
        return 0

    lax.fori_loop(0, S - 1, greet_str, 0)
    lax.fori_loop(0, F - 1, greet_fac, 0)

    for s in range(K):
        wb[pl.ds(s * T, T), :] = btab[btile[fac, s]].T
        wa[:, pl.ds(s * T, T)] = atab[atile[fac, s]]

    def sign(k, _):
        load(k).wait()
        amp[k] = amp[k] * sign_b[k] * sign_a[...]
        return 0

    lax.fori_loop(0, NB, sign, 0)
    pl.semaphore_wait(barrier, S + F - 2)

    mid = S // 2

    def dest(t):
        side = (me // mid + 1 + t // mid) % 2
        return side * mid + (me + 1 + t) % mid

    def beta(q, c):
        j = q * C + c
        lhs = jnp.concatenate([amp[bidx[fac, j, s]] for s in range(K)], axis=1)
        res = jnp.dot(lhs, wb[...], preferred_element_type=jnp.float32)
        return res.astype(jnp.bfloat16).reshape(A, T, T)

    def str_copy(c, q, src):
        return pltpu.make_async_remote_copy(
            src_ref=half_send.at[c, q],
            dst_ref=recv[c].at[pl.ds(src * A, A)],
            send_sem=s_send.at[c, q],
            recv_sem=s_recv.at[c, src],
            device_id={"str": q},
            device_id_type=MESH,
        )

    for c in range(C):

        def step(t, _):
            q = dest(t)
            half_send[c, q] = beta(q, c)
            str_copy(c, q, me).start()
            return 0

        lax.fori_loop(0, S - 1, step, 0)
        recv[c][pl.ds(me * A, A)] = beta(me, c)

    def fac_target(g):
        return ((fac + 1 + g // 2) % NF) * 2 + (part + 1 + g % 2) % 2

    def fac_copy(c, p, src_fac, src_part):
        return pltpu.make_async_remote_copy(
            src_ref=term_send.at[c, pl.ds(p * per, per)],
            dst_ref=out.at[src_fac, src_part, :, pl.ds(c * T, T)],
            send_sem=f_send.at[c, p],
            recv_sem=f_recv.at[c, src_fac * 2 + src_part],
            device_id={"fac": p},
            device_id_type=MESH,
        )

    def own_copy(c):
        return pltpu.make_async_copy(
            term_send.at[c, pl.ds(pos * per, per)],
            out.at[fac, part, :, pl.ds(c * T, T)],
            f_send.at[c, pos],
        )

    for c in range(C):

        def arrive(t, _):
            src = (me + 1 + t) % S
            str_copy(c, src, src).wait_recv()
            return 0

        lax.fori_loop(0, S - 1, arrive, 0)

        def rows_of(p):
            def block(b, _):
                i = p * (per // T) + b
                rhs = jnp.concatenate([recv[c][aidx[fac, i, s]] for s in range(K)], axis=0)
                res = jnp.dot(wa[...], rhs, preferred_element_type=jnp.float32)
                term_send[c, pl.ds(pl.multiple_of(i * T, T), T), :] = res.astype(jnp.bfloat16)
                return 0

            lax.fori_loop(0, per // T, block, 0)

        def group(g, _):
            p = fac_target(g)
            rows_of(p)
            fac_copy(c, p, fac, part).start()
            return 0

        lax.fori_loop(0, F - 1, group, 0)
        rows_of(pos)
        own_copy(c).start()

    for c in range(C):

        def finish_str(t, _):
            q = (me + 1 + t) % S
            str_copy(c, q, me).wait_send()
            return 0

        lax.fori_loop(0, S - 1, finish_str, 0)

        def finish_fac(t, _):
            p = (pos + 1 + t) % F
            fac_copy(c, p, fac, part).wait_send()
            fac_copy(c, p, p // 2, p % 2).wait_recv()
            return 0

        lax.fori_loop(0, F - 1, finish_fac, 0)
        own_copy(c).wait()


def local(S, F, amplitudes, beta_index, beta_tile, beta_flip, alpha_index, alpha_tile, alpha_flip, beta_tiles, alpha_tiles):
    NF, NB, K = beta_index.shape
    T = beta_tiles.shape[1]
    parts, height, width = amplitudes.shape
    total = height * S
    A = height // T
    C = width // S // T
    pos = lax.axis_index("fac")
    me = lax.axis_index("str")
    bflip = lax.dynamic_index_in_dim(beta_flip, pos // 2, 0, keepdims=False)
    aflip = lax.dynamic_slice(alpha_flip, (pos // 2, me * height), (1, height))[0]
    sign_b = (1 - 2 * bflip).astype(jnp.bfloat16).reshape(NB, 1, T)
    sign_a = jnp.broadcast_to((1 - 2 * aflip).astype(jnp.bfloat16)[:, None], (height, T))
    dims = (S, F, NF, C, A, T, K)
    vmem = pl.BlockSpec(memory_space=pltpu.VMEM)
    smem = pl.BlockSpec(memory_space=pltpu.SMEM)
    terms = pl.pallas_call(
        functools.partial(kernel, dims),
        out_shape=jax.ShapeDtypeStruct((NF, parts, total // F, width // S), jnp.bfloat16),
        in_specs=[pl.BlockSpec(memory_space=pl.ANY), vmem, vmem, smem, smem, smem, smem, vmem, vmem],
        out_specs=pl.BlockSpec(memory_space=pl.ANY),
        scratch_shapes=[
            pltpu.VMEM((NB, height, T), jnp.bfloat16),
            pltpu.VMEM((C, S, A, T, T), jnp.bfloat16),
            pltpu.VMEM((C, total, T), jnp.bfloat16),
            pltpu.VMEM((K * T, T), jnp.bfloat16),
            pltpu.VMEM((T, K * T), jnp.bfloat16),
        ]
        + [pltpu.VMEM((NB, T, T), jnp.bfloat16) for _ in range(C)]
        + [
            pltpu.SemaphoreType.DMA((NB,)),
            pltpu.SemaphoreType.DMA((C, S)),
            pltpu.SemaphoreType.DMA((C, S)),
            pltpu.SemaphoreType.DMA((C, F)),
            pltpu.SemaphoreType.DMA((C, F)),
        ],
        compiler_params=pltpu.CompilerParams(collective_id=0, has_side_effects=True, vmem_limit_bytes=48 * 1024 * 1024),
        name="sigma",
    )(amplitudes, sign_b, sign_a, beta_index, beta_tile, alpha_index, alpha_tile, beta_tiles, alpha_tiles)
    return jnp.sum(terms.astype(jnp.float32), axis=0)


def solution(mesh):
    return jax.shard_map(
        functools.partial(local, mesh.shape["str"], mesh.shape["fac"]),
        mesh=mesh,
        in_specs=(P(None, "str", None), P(), P(), P(), P(), P(), P(), P(), P()),
        out_specs=P(None, "fac", "str"),
        check_vma=False,
    )
```

time: 446 us -> 127 us (0.28)
  waiting for transfers between devices: 163 us -> 0 us
  local copies, waits for them, and re-layouts: 161 us -> 5.15 us
  Pallas kernels: 0 us -> 117 us
  matrix products: 52.9 us -> 0 us
  other arithmetic: 47.1 us -> 4.35 us
  between operations: 13.7 us -> 0.03 us
  starting transfers between devices: 7.29 us -> 0 us
    pallas_call x0 -> x1, Pallas kernels: none -> 117 us  [local(): pl.pallas_call(functools.partial(kernel, dims), out_shape=jax.ShapeDtypeS...]
    all_to_all x1 -> x0, waiting for transfers between devices: 91.7 us -> none  [local(): lax.all_to_all(half, 'str', split_axis=2, concat_axis=1, tiled=True)]
    gather x10 -> x0, local copies, waits for them, and re-layouts: 73.2 us -> none  [the longest x4 36 us: apply_beta(): gathered = blocks[:, :, chosen]]
    reduce_scatter x1 -> x0, waiting for transfers between devices: 70.8 us -> none  [local(): lax.psum_scatter(padded.astype(jnp.bfloat16), 'fac', scatter_dimension=1,...]
    dot_general x8 -> x0, matrix products: 52.9 us -> none  [the longest x4 31.6 us: apply_beta(): jnp.einsum('pajkc,krc->pajr', gathered, weights, preferred_element_type=j...]
    reshape x2 -> x0, local copies, waits for them, and re-layouts: 42.9 us -> none  [the longest x1 36.5 us: apply_beta(): jnp.concatenate(pieces, axis=2).reshape(part_count, height, column_count)]
    unnamed x1 -> x0, other arithmetic: 28.5 us -> none
    unnamed x41 -> x10, local copies, waits for them, and re-layouts: 33.3 us -> 5.02 us
  transfers between devices with their start and end apart: 2 -> 0, of which waited for: 2 -> 0; matrix products, arithmetic and copies ran while one was open for 0% -> 0% of each run, Pallas kernels for 0% -> 0%
where the time goes in v1:
time: 127 us; the launch traced here: 126 us
  Pallas kernels  117 us (92%)
  local copies, waits for them, and re-layouts  5.15 us (4%)
  other arithmetic  4.35 us (3%)
    pallas_call x1, Pallas kernels, local(): pl.pallas_call(functools.partial(kernel, dims), out_shape=jax.ShapeDtypeS...  117 us
    unnamed x10, local copies, waits for them, and re-layouts  5.02 us
    reduce_sum x1, other arithmetic, local(): return jnp.sum(terms.astype(jnp.float32), axis=0)  2.78 us

profile of v1, /device:TPU:0, one launch (start us, length us, event | category | flops | bytes accessed | tf_op | source)
XLA Modules:
  0.0 126.2 jit_solution(6695290041646592630)
XLA Ops:
  0.0 0.8 convert_reduce_fusion.1
  0.8 0.8 convert_bitcast_fusion.sign_b
  1.6 0.8 copy.10.bidx
  2.4 0.8 copy.11.aidx
  3.2 0.1 broadcast_in_dim.2.sign_a
  3.3 0.0 copy-start
  3.3 1.0 copy-done
  4.3 0.0 copy-start.1
  4.3 1.0 copy-done.1
  5.4 0.0 copy-start.2
  5.4 0.7 copy-done.2
  6.1 0.0 copy-start.3
  6.1 0.7 copy-done.3
  6.7 116.6 %sigma.1 = bf16[2,2,1024,512]{3,2,1,0:T(8,128)(2,1)S(1)} custom-call(bf16[2,512,4096]{2,1,0:T(8,128)(2,1)} %amp_hbm.1, bf16[32,1,128]{2,1,0:T(2,128)(2,1)S(1)} %convert_bitcast_fusion.sign_b, bf16[512,128]{1,0:T(8,128)(2,1)S(1)} %broadcast_in_dim.2.sign_a, s32[2,32,12]{2,1,0:T(8,128)S(1)} %copy.10.bidx, s32[2,12]{1,0:T(2,128)S(1)} %copy-done.2, ...), custom_call_target="tpu_custom_call" | custom-call | tf_op jit(solution)/shard_map/sigma/pallas_call | solution.py:177
  123.4 2.8 %convert_reduce_fusion = f32[2,1024,512]{2,1,0:T(8,128)} fusion(bf16[2,2,1024,512]{3,2,1,0:T(8,128)(2,1)S(1)} %sigma.1), kind=kLoop, calls=%fused_computation | loop fusion | flops 3145728 | bytes 8388608 | tf_op jit(solution)/shard_map/reduce_sum | solution.py:200
Async XLA Ops:
  3.3 1.0 copy-start
  4.3 1.0 copy-start.1
  5.4 0.7 copy-start.2
  6.1 0.7 copy-start.3

commit v2 on v1

v2 whole, which is shorter than its diff:
```python
import functools

import jax
import jax.numpy as jnp
from jax import lax
from jax.experimental import pallas as pl
from jax.experimental.pallas import tpu as pltpu
from jax.sharding import PartitionSpec as P

MESH = pl.DeviceIdType.MESH


def split_position(pos, F):
    factors = F // 2
    return pos % factors, pos // factors


def kernel(dims, amp_hbm, bflip_hbm, aflip_hbm, btab_hbm, atab_hbm, ids, out, *scratch):
    S, F, C, A, T, K, NB = dims
    amp, half_send, term_send, pair_recv, wb, wa, bflip, aflip, btab, atab, sign_a = scratch[:11]
    recv = scratch[11 : 11 + C]
    a_sem, t_sem, s_send, s_recv, p_send, p_recv, f_send, f_recv = scratch[11 + C :]
    me = lax.axis_index("str")
    pos = lax.axis_index("fac")
    fac, part = split_position(pos, F)
    chips = F // 2
    chip = pos // 2
    core = pos % 2
    per = term_send.shape[1] // F

    barrier = pltpu.get_barrier_semaphore()

    def greet_str(t, _):
        pl.semaphore_signal(barrier, inc=1, device_id={"str": (me + 1 + t) % S}, device_id_type=MESH)
        return 0

    def greet_fac(t, _):
        peer = ((chip + 1 + t) % chips) * 2 + core
        pl.semaphore_signal(barrier, inc=1, device_id={"fac": peer}, device_id_type=MESH)
        return 0

    partner = chip * 2 + 1 - core
    lax.fori_loop(0, S - 1, greet_str, 0)
    lax.fori_loop(0, chips - 1, greet_fac, 0)
    pl.semaphore_signal(barrier, inc=1, device_id={"fac": partner}, device_id_type=MESH)

    tables = [
        pltpu.make_async_copy(src, dst, t_sem.at[n])
        for n, (src, dst) in enumerate([(bflip_hbm, bflip), (aflip_hbm, aflip), (btab_hbm, btab), (atab_hbm, atab)])
    ]

    def load(k):
        return pltpu.make_async_copy(amp_hbm.at[part, :, pl.ds(pl.multiple_of(k * T, T), T)], amp.at[k], a_sem.at[k])

    def start_load(k, _):
        load(k).start()
        return 0

    for copy in tables[:3]:
        copy.start()
    lax.fori_loop(0, NB, start_load, 0)
    tables[3].start()

    def signs(flips, block):
        value = flips[:, pl.ds(pl.multiple_of(block * T, T), T)].astype(jnp.float32)
        mine = lax.broadcasted_iota(jnp.int32, value.shape, 0) == fac
        return 1 - 2 * jnp.sum(jnp.where(mine, value, 0.0), axis=0, keepdims=True)

    tables[1].wait()
    for r in range(A):
        row = signs(aflip, me * A + r)
        sign_a[pl.ds(r * T, T), :] = jnp.broadcast_to(row, (T, T)).T.astype(jnp.bfloat16)
    tables[2].wait()
    for s in range(K):
        wb[pl.ds(s * T, T), :] = btab[ids[2 * K, s]].T
    tables[0].wait()

    def sign(k, _):
        load(k).wait()
        amp[k] = amp[k] * signs(bflip, k).astype(jnp.bfloat16) * sign_a[...]
        return 0

    lax.fori_loop(0, NB, sign, 0)
    pl.semaphore_wait(barrier, S - 1 + chips)

    mid = S // 2

    def dest(t):
        side = (me // mid + 1 + t // mid) % 2
        return side * mid + (me + 1 + t) % mid

    def beta(q, c):
        j = q * C + c
        lhs = jnp.concatenate([amp[ids[s, j]] for s in range(K)], axis=1)
        res = jnp.dot(lhs, wb[...], preferred_element_type=jnp.float32)
        return res.astype(jnp.bfloat16).reshape(A, T, T)

    def str_copy(c, q, src):
        return pltpu.make_async_remote_copy(
            src_ref=half_send.at[c, q],
            dst_ref=recv[c].at[pl.ds(src * A, A)],
            send_sem=s_send.at[c, q],
            recv_sem=s_recv.at[c, src],
            device_id={"str": q},
            device_id_type=MESH,
        )

    for c in range(C):

        def step(t, _):
            q = dest(t)
            half_send[c, q] = beta(q, c)
            str_copy(c, q, me).start()
            return 0

        lax.fori_loop(0, S - 1, step, 0)
        recv[c][pl.ds(me * A, A)] = beta(me, c)

    tables[3].wait()
    for s in range(K):
        wa[:, pl.ds(s * T, T)] = atab[ids[2 * K + 1, s]]

    def pair_copy(c, y, owner):
        return pltpu.make_async_remote_copy(
            src_ref=term_send.at[c, pl.ds((y * 2 + owner) * per, per)],
            dst_ref=pair_recv.at[c, y],
            send_sem=p_send.at[c, y],
            recv_sem=p_recv.at[c, y],
            device_id={"fac": partner},
            device_id_type=MESH,
        )

    def fac_copy(c, y, src):
        src_fac, src_part = split_position(src, F)
        return pltpu.make_async_remote_copy(
            src_ref=term_send.at[c, pl.ds((y * 2 + core) * per, per)],
            dst_ref=out.at[src_fac // 2, src_part, :, pl.ds(c * T, T)],
            send_sem=f_send.at[c, y],
            recv_sem=f_recv.at[c, src // 2],
            device_id={"fac": y * 2 + core},
            device_id_type=MESH,
        )

    def own_copy(c):
        return pltpu.make_async_copy(
            term_send.at[c, pl.ds(pos * per, per)],
            out.at[fac // 2, part, :, pl.ds(c * T, T)],
            f_send.at[c, chip],
        )

    for c in range(C):

        def arrive(t, _):
            src = (me + 1 + t) % S
            str_copy(c, src, src).wait_recv()
            return 0

        lax.fori_loop(0, S - 1, arrive, 0)

        def alpha(i):
            rhs = jnp.concatenate([recv[c][ids[K + s, i]] for s in range(K)], axis=0)
            return jnp.dot(wa[...], rhs, preferred_element_type=jnp.float32)

        def store(i, value):
            term_send[c, pl.ds(pl.multiple_of(i * T, T), T), :] = value.astype(jnp.bfloat16)

        def for_partner(y):
            def block(b, _):
                i = (y * 2 + 1 - core) * (per // T) + b
                store(i, alpha(i))
                return 0

            lax.fori_loop(0, per // T, block, 0)
            pair_copy(c, y, 1 - core).start()

        def for_self(y):
            pair_copy(c, y, core).wait_recv()

            def block(b, _):
                i = (y * 2 + core) * (per // T) + b
                other = pair_recv[c, y, pl.ds(pl.multiple_of(b * T, T), T), :]
                store(i, alpha(i) + other.astype(jnp.float32))
                return 0

            lax.fori_loop(0, per // T, block, 0)

        def group(g, _):
            y = (chip + 1 + g) % chips
            for_partner(y)
            for_self(y)
            fac_copy(c, y, pos).start()
            return 0

        lax.fori_loop(0, chips - 1, group, 0)
        for_partner(chip)
        for_self(chip)
        own_copy(c).start()

    for c in range(C):

        def finish_str(t, _):
            str_copy(c, (me + 1 + t) % S, me).wait_send()
            return 0

        lax.fori_loop(0, S - 1, finish_str, 0)

        def finish_pair(y, _):
            pair_copy(c, y, 1 - core).wait_send()
            return 0

        lax.fori_loop(0, chips, finish_pair, 0)

        def finish_fac(t, _):
            y = (chip + 1 + t) % chips
            fac_copy(c, y, pos).wait_send()
            fac_copy(c, y, y * 2 + core).wait_recv()
            return 0

        lax.fori_loop(0, chips - 1, finish_fac, 0)
        own_copy(c).wait()


def local(S, F, amplitudes, beta_index, beta_tile, beta_flip, alpha_index, alpha_tile, alpha_flip, beta_tiles, alpha_tiles):
    NF, NB, K = beta_index.shape
    NT, T, _ = beta_tiles.shape
    parts, height, width = amplitudes.shape
    total = height * S
    A = height // T
    C = width // S // T
    assert F == 2 * NF and parts == 2 and NF % 2 == 0 and K <= NB
    per = total // F
    fac, _ = split_position(lax.axis_index("fac"), F)
    lists = [lax.dynamic_index_in_dim(x.transpose(2, 0, 1), fac, 1, keepdims=False) for x in (beta_index, alpha_index)]
    kinds = [lax.dynamic_slice(x, (fac, 0), (1, K)) for x in (beta_tile, alpha_tile)]
    ids = jnp.concatenate(lists + [jnp.pad(x, ((0, 0), (0, NB - K))) for x in kinds], axis=0)
    hbm = pl.BlockSpec(memory_space=pl.ANY)
    bf16 = jnp.bfloat16
    dma = pltpu.SemaphoreType.DMA
    terms = pl.pallas_call(
        functools.partial(kernel, (S, F, C, A, T, K, NB)),
        out_shape=jax.ShapeDtypeStruct((NF // 2, parts, per, width // S), bf16),
        in_specs=[hbm] * 5 + [pl.BlockSpec(memory_space=pltpu.SMEM)],
        out_specs=hbm,
        scratch_shapes=[
            pltpu.VMEM((NB, height, T), bf16),
            pltpu.VMEM((C, S, A, T, T), bf16),
            pltpu.VMEM((C, total, T), bf16),
            pltpu.VMEM((C, F // 2, per, T), bf16),
            pltpu.VMEM((K * T, T), bf16),
            pltpu.VMEM((T, K * T), bf16),
            pltpu.VMEM((NF, width), jnp.int32),
            pltpu.VMEM((NF, total), jnp.int32),
            pltpu.VMEM((NT, T, T), bf16),
            pltpu.VMEM((NT, T, T), bf16),
            pltpu.VMEM((height, T), bf16),
        ]
        + [pltpu.VMEM((NB, T, T), bf16) for _ in range(C)]
        + [dma((NB,)), dma((4,)), dma((C, S)), dma((C, S))]
        + [dma((C, F // 2)) for _ in range(4)],
        compiler_params=pltpu.CompilerParams(collective_id=0, has_side_effects=True, vmem_limit_bytes=67043328),
        name="sigma",
    )(amplitudes, beta_flip, alpha_flip, beta_tiles, alpha_tiles, ids)
    return jnp.sum(terms.astype(jnp.float32), axis=0)


def solution(mesh):
    return jax.shard_map(
        functools.partial(local, mesh.shape["str"], mesh.shape["fac"]),
        mesh=mesh,
        in_specs=(P(None, "str", None), P(), P(), P(), P(), P(), P(), P(), P()),
        out_specs=P(None, "fac", "str"),
        check_vma=False,
    )
```

time: 127 us -> 121 us (0.953)
  local copies, waits for them, and re-layouts: 5.15 us -> 1.44 us
  Pallas kernels: 117 us -> 114 us
    unnamed x10 -> x2, local copies, waits for them, and re-layouts: 5.02 us -> 0.01 us
    pallas_call x1, Pallas kernels: 117 us -> 114 us  [local(): pl.pallas_call(functools.partial(kernel, (S, F, C, A, T, K, NB)), out_sha...]
    convert_element_type x2 -> x0, other arithmetic: 1.57 us -> none  [the longest x1 0.79 us: local(): sign_b = (1 - 2 * bflip).astype(jnp.bfloat16).reshape(NB, 1, T)]
    reduce_sum x1, other arithmetic: 2.78 us -> 4.2 us  [local(): return jnp.sum(terms.astype(jnp.float32), axis=0)]
where the time goes in v2:
time: 121 us; the launch traced here: 120 us
  Pallas kernels  114 us (94%)
  other arithmetic  4.81 us (4%)
  local copies, waits for them, and re-layouts  1.44 us (1%)
    pallas_call x1, Pallas kernels, local(): pl.pallas_call(functools.partial(kernel, (S, F, C, A, T, K, NB)), out_sha...  114 us
    reduce_sum x1, other arithmetic, local(): return jnp.sum(terms.astype(jnp.float32), axis=0)  4.2 us

profile of v2, /device:TPU:0, one launch (start us, length us, event | category | flops | bytes accessed | tf_op | source)
XLA Modules:
  0.0 120.1 jit_solution(10370150997873301044)
XLA Ops:
  0.0 0.7 constant_dynamic-slice_fusion
  0.7 0.7 constant_dynamic-slice_fusion.2
  1.5 0.6 pad_add_fusion.ids
  2.1 113.8 %sigma.1 = bf16[1,2,1024,512]{3,2,1,0:T(8,128)(2,1)} custom-call(bf16[2,512,4096]{2,1,0:T(8,128)(2,1)} %amp_hbm.1, s32[2,4096]{1,0:T(2,128)} %bflip_hbm.1, s32[2,4096]{1,0:T(2,128)} %aflip_hbm.1, bf16[16,128,128]{2,1,0:T(8,128)(2,1)} %btab_hbm.1, bf16[16,128,128]{2,1,0:T(8,128)(2,1)} %atab_hbm.1, s32[26,32]{1,0:T(8,128)} %pad_add_fusion.ids), custom_call_target="tpu_custom_call" | custom-call | tf_op jit(solution)/shard_map/sigma/pallas_call | solution.py:239
  115.9 4.2 %bitcast_convert_fusion = f32[2,1024,512]{2,1,0:T(8,128)} fusion(bf16[1,2,1024,512]{3,2,1,0:T(8,128)(2,1)} %sigma.1), kind=kLoop, calls=%fused_computation | loop fusion | flops 1048576 | bytes 6291456 | tf_op jit(solution)/shard_map/reduce_sum | solution.py:263
  (2 shorter events, 0.0 us)

commit v3 on v2

v3 whole, which is shorter than its diff:
```python
import functools
import math

import jax
import jax.numpy as jnp
from jax import lax
from jax.experimental import pallas as pl
from jax.experimental.pallas import tpu as pltpu
from jax.sharding import PartitionSpec as P

MESH = pl.DeviceIdType.MESH


def split_position(pos, F):
    factors = F // 2
    return pos % factors, pos // factors


def kernel(dims, amp_hbm, bflip_hbm, aflip_hbm, btab_hbm, atab_hbm, bidx_hbm, aidx_hbm, btile_hbm, atile_hbm, out, *scratch):
    S, F, C, A, T, K, NB, H = dims
    amp, half_send, term_send, pair_recv, wb, wa, bflip, aflip, btab, atab, sign_a, bidx, aidx, btile, atile = scratch[:15]
    recv = scratch[15 : 15 + C]
    a_sem, t_sem, s_send, s_recv, p_send, p_recv, f_send, f_recv = scratch[15 + C :]
    me = lax.axis_index("str")
    pos = lax.axis_index("fac")
    fac, part = split_position(pos, F)
    chips = F // 2
    chip = pos // 2
    core = pos % 2
    per = term_send.shape[1] // F

    barrier = pltpu.get_barrier_semaphore()

    def greet_str(t, _):
        pl.semaphore_signal(barrier, inc=1, device_id={"str": (me + 1 + t) % S}, device_id_type=MESH)
        return 0

    def greet_fac(t, _):
        peer = ((chip + 1 + t) % chips) * 2 + core
        pl.semaphore_signal(barrier, inc=1, device_id={"fac": peer}, device_id_type=MESH)
        return 0

    partner = chip * 2 + 1 - core
    lax.fori_loop(0, S - 1, greet_str, 0)
    lax.fori_loop(0, chips - 1, greet_fac, 0)
    pl.semaphore_signal(barrier, inc=1, device_id={"fac": partner}, device_id_type=MESH)

    tables = [
        pltpu.make_async_copy(src, dst, t_sem.at[n])
        for n, (src, dst) in enumerate(
            [
                (bflip_hbm, bflip),
                (aflip_hbm, aflip),
                (btab_hbm, btab),
                (bidx_hbm, bidx),
                (btile_hbm, btile),
                (atab_hbm, atab),
                (aidx_hbm, aidx),
                (atile_hbm, atile),
            ]
        )
    ]

    def load(k):
        return pltpu.make_async_copy(amp_hbm.at[part, :, pl.ds(pl.multiple_of(k * T, T), T)], amp.at[k], a_sem.at[k])

    def start_load(k, _):
        load(k).start()
        return 0

    for copy in tables[:5]:
        copy.start()
    lax.fori_loop(0, NB, start_load, 0)
    for copy in tables[5:]:
        copy.start()

    def signs(flips, block):
        value = flips[:, pl.ds(pl.multiple_of(block * T, T), T)].astype(jnp.float32)
        mine = lax.broadcasted_iota(jnp.int32, value.shape, 0) == fac
        return 1 - 2 * jnp.sum(jnp.where(mine, value, 0.0), axis=0, keepdims=True)

    tables[1].wait()
    for r in range(A):
        row = signs(aflip, me * A + r)
        sign_a[pl.ds(r * T, T), :] = jnp.broadcast_to(row, (T, T)).T.astype(jnp.bfloat16)
    tables[4].wait()
    tables[2].wait()
    for s in range(K):
        wb[pl.ds(s * T, T), :] = btab[btile[fac, s]].T
    tables[0].wait()
    tables[3].wait()

    def sign(k, _):
        load(k).wait()
        amp[k] = amp[k] * signs(bflip, k).astype(jnp.bfloat16) * sign_a[...]
        return 0

    lax.fori_loop(0, NB, sign, 0)
    pl.semaphore_wait(barrier, S - 1 + chips)

    mid = S // 2

    def dest(t):
        side = (me // mid + 1 + t // mid) % 2
        return side * mid + (me + 1 + t) % mid

    def beta(q, c):
        j = q * C + c
        lhs = jnp.concatenate([amp[bidx[s, fac, j]] for s in range(K)], axis=1)
        res = jnp.dot(lhs, wb[...], preferred_element_type=jnp.float32)
        return res.astype(jnp.bfloat16).reshape(A, T, T)

    def str_copy(c, q, src):
        return pltpu.make_async_remote_copy(
            src_ref=half_send.at[c, q],
            dst_ref=recv[c].at[pl.ds(src * A, A)],
            send_sem=s_send.at[c, q],
            recv_sem=s_recv.at[c, src],
            device_id={"str": q},
            device_id_type=MESH,
        )

    for c in range(C):

        def step(t, _):
            q = dest(t)
            half_send[c, q] = beta(q, c)
            str_copy(c, q, me).start()
            return 0

        lax.fori_loop(0, S - 1, step, 0)
        recv[c][pl.ds(me * A, A)] = beta(me, c)

    for copy in tables[5:]:
        copy.wait()
    for s in range(K):
        wa[:, pl.ds(s * T, T)] = atab[atile[fac, s]]

    piece = per // H
    groups = chips * H

    def place(g):
        return (chip + 1 + g // H) % chips, g % H

    def pair_copy(c, y, h, owner):
        return pltpu.make_async_remote_copy(
            src_ref=term_send.at[c, pl.ds((y * 2 + owner) * per + h * piece, piece)],
            dst_ref=pair_recv.at[c, y, h],
            send_sem=p_send.at[c, y, h],
            recv_sem=p_recv.at[c, y, h],
            device_id={"fac": partner},
            device_id_type=MESH,
        )

    def fac_copy(c, y, h, src):
        src_fac, src_part = split_position(src, F)
        return pltpu.make_async_remote_copy(
            src_ref=term_send.at[c, pl.ds((y * 2 + core) * per + h * piece, piece)],
            dst_ref=out.at[src_fac // 2, src_part, pl.ds(h * piece, piece), pl.ds(c * T, T)],
            send_sem=f_send.at[c, y, h],
            recv_sem=f_recv.at[c, src // 2, h],
            device_id={"fac": y * 2 + core},
            device_id_type=MESH,
        )

    def own_copy(c):
        return pltpu.make_async_copy(
            term_send.at[c, pl.ds(pos * per, per)],
            out.at[fac // 2, part, :, pl.ds(c * T, T)],
            f_send.at[c, chip, 0],
        )

    for c in range(C):

        def arrive(t, _):
            src = (me + 1 + t) % S
            str_copy(c, src, src).wait_recv()
            return 0

        lax.fori_loop(0, S - 1, arrive, 0)

        def alpha(i):
            rhs = jnp.concatenate([recv[c][aidx[s, fac, i]] for s in range(K)], axis=0)
            return jnp.dot(wa[...], rhs, preferred_element_type=jnp.float32)

        def store(i, value):
            term_send[c, pl.ds(pl.multiple_of(i * T, T), T), :] = value.astype(jnp.bfloat16)

        def for_partner(g):
            y, h = place(g)

            def block(b, _):
                i = (y * 2 + 1 - core) * (per // T) + h * (piece // T) + b
                store(i, alpha(i))
                return 0

            lax.fori_loop(0, piece // T, block, 0)
            pair_copy(c, y, h, 1 - core).start()

        def for_self(g):
            y, h = place(g)
            pair_copy(c, y, h, core).wait_recv()

            def block(b, _):
                i = (y * 2 + core) * (per // T) + h * (piece // T) + b
                other = pair_recv[c, y, h, pl.ds(pl.multiple_of(b * T, T), T), :]
                store(i, alpha(i) + other.astype(jnp.float32))
                return 0

            lax.fori_loop(0, piece // T, block, 0)

        def away(g, _):
            for_partner(g + 1)
            for_self(g)
            y, h = place(g)
            fac_copy(c, y, h, pos).start()
            return 0

        def home(g, _):
            for_partner(g + 1)
            for_self(g)
            return 0

        for_partner(0)
        lax.fori_loop(0, groups - H, away, 0)
        lax.fori_loop(groups - H, groups - 1, home, 0)
        for_self(groups - 1)
        own_copy(c).start()

    for c in range(C):

        def finish_str(t, _):
            str_copy(c, (me + 1 + t) % S, me).wait_send()
            return 0

        lax.fori_loop(0, S - 1, finish_str, 0)

        def finish_pair(g, _):
            y, h = place(g)
            pair_copy(c, y, h, 1 - core).wait_send()
            return 0

        lax.fori_loop(0, groups, finish_pair, 0)

        def finish_fac(g, _):
            y, h = place(g)
            fac_copy(c, y, h, pos).wait_send()
            fac_copy(c, y, h, y * 2 + core).wait_recv()
            return 0

        lax.fori_loop(0, groups - H, finish_fac, 0)
        own_copy(c).wait()


def local(S, F, amplitudes, beta_index, beta_tile, beta_flip, alpha_index, alpha_tile, alpha_flip, beta_tiles, alpha_tiles):
    NF, NB, K = beta_index.shape
    NT, T, _ = beta_tiles.shape
    parts, height, width = amplitudes.shape
    total = height * S
    A = height // T
    C = width // S // T
    assert F == 2 * NF and parts == 2 and NF % 2 == 0 and K <= NB
    per = total // F
    H = math.gcd(per // T, 4)
    ids = (beta_index.transpose(2, 0, 1), alpha_index.transpose(2, 0, 1), beta_tile, alpha_tile)
    hbm = pl.BlockSpec(memory_space=pltpu.HBM)
    bf16 = jnp.bfloat16
    dma = pltpu.SemaphoreType.DMA
    terms = pl.pallas_call(
        functools.partial(kernel, (S, F, C, A, T, K, NB, H)),
        out_shape=jax.ShapeDtypeStruct((NF // 2, parts, per, width // S), bf16),
        in_specs=[hbm] * 9,
        out_specs=pl.BlockSpec(memory_space=pl.ANY),
        scratch_shapes=[
            pltpu.VMEM((NB, height, T), bf16),
            pltpu.VMEM((C, S, A, T, T), bf16),
            pltpu.VMEM((C, total, T), bf16),
            pltpu.VMEM((C, F // 2, H, per // H, T), bf16),
            pltpu.VMEM((K * T, T), bf16),
            pltpu.VMEM((T, K * T), bf16),
            pltpu.VMEM((NF, width), jnp.int32),
            pltpu.VMEM((NF, total), jnp.int32),
            pltpu.VMEM((NT, T, T), bf16),
            pltpu.VMEM((NT, T, T), bf16),
            pltpu.VMEM((height, T), bf16),
            pltpu.SMEM((K, NF, NB), jnp.int32),
            pltpu.SMEM((K, NF, NB), jnp.int32),
            pltpu.SMEM((NF, K), jnp.int32),
            pltpu.SMEM((NF, K), jnp.int32),
        ]
        + [pltpu.VMEM((NB, T, T), bf16) for _ in range(C)]
        + [dma((NB,)), dma((8,)), dma((C, S)), dma((C, S))]
        + [dma((C, F // 2, H)) for _ in range(4)],
        compiler_params=pltpu.CompilerParams(collective_id=0, has_side_effects=True, vmem_limit_bytes=67043328),
        name="sigma",
    )(amplitudes, beta_flip, alpha_flip, beta_tiles, alpha_tiles, *ids)
    return jnp.sum(terms.astype(jnp.float32), axis=0)


def solution(mesh):
    return jax.shard_map(
        functools.partial(local, mesh.shape["str"], mesh.shape["fac"]),
        mesh=mesh,
        in_specs=(P(None, "str", None), P(), P(), P(), P(), P(), P(), P(), P()),
        out_specs=P(None, "fac", "str"),
        check_vma=False,
    )
```

time: 121 us -> 116 us (0.959)
  Pallas kernels: 114 us -> 112 us
  local copies, waits for them, and re-layouts: 1.44 us -> 0 us
    pallas_call x1, Pallas kernels: 114 us -> 112 us  [local(): pl.pallas_call(functools.partial(kernel, (S, F, C, A, T, K, NB, H)), out_...]
where the time goes in v3:
time: 116 us
  Pallas kernels  112 us (97%)
  other arithmetic  4.2 us (4%)
    pallas_call x1, Pallas kernels, local(): pl.pallas_call(functools.partial(kernel, (S, F, C, A, T, K, NB, H)), out_...  112 us
    reduce_sum x1, other arithmetic, local(): return jnp.sum(terms.astype(jnp.float32), axis=0)  4.2 us

profile of v3, /device:TPU:0, one launch (start us, length us, event | category | flops | bytes accessed | tf_op | source)
XLA Modules:
  0.0 116.0 jit_solution(12243423750111168645)
XLA Ops:
  0.0 111.8 %sigma.1 = bf16[1,2,1024,512]{3,2,1,0:T(8,128)(2,1)} custom-call(bf16[2,512,4096]{2,1,0:T(8,128)(2,1)} %amp_hbm.1, s32[2,4096]{1,0:T(2,128)} %bflip_hbm.1, s32[2,4096]{1,0:T(2,128)} %aflip_hbm.1, bf16[16,128,128]{2,1,0:T(8,128)(2,1)} %btab_hbm.1, bf16[16,128,128]{2,1,0:T(8,128)(2,1)} %atab_hbm.1, s32[12,2,32]{2,1,0:T(2,128)} %bitcast.5, ...), custom_call_target="tpu_custom_call" | custom-call | tf_op jit(solution)/shard_map/sigma/pallas_call | solution.py:269
  111.8 4.2 %bitcast_convert_fusion = f32[2,1024,512]{2,1,0:T(8,128)} fusion(bf16[1,2,1024,512]{3,2,1,0:T(8,128)(2,1)} %sigma.1), kind=kLoop, calls=%fused_computation | loop fusion | flops 1048576 | bytes 6291456 | tf_op jit(solution)/shard_map/reduce_sum | solution.py:297

commit v4 on v3

--- a/solution.py
+++ b/solution.py
@@ -18,9 +18,9 @@
 
 def kernel(dims, amp_hbm, bflip_hbm, aflip_hbm, btab_hbm, atab_hbm, bidx_hbm, aidx_hbm, btile_hbm, atile_hbm, out, *scratch):
     S, F, C, A, T, K, NB, H = dims
-    amp, half_send, term_send, pair_recv, wb, wa, bflip, aflip, btab, atab, sign_a, bidx, aidx, btile, atile = scratch[:15]
-    recv = scratch[15 : 15 + C]
-    a_sem, t_sem, s_send, s_recv, p_send, p_recv, f_send, f_recv = scratch[15 + C :]
+    amp, half_send, term_send, pair_recv, wb, wa, bflip, aflip, btab, atab, sign_a, bidx, aidx, btile, atile, raw = scratch[:16]
+    recv = scratch[16 : 16 + C]
+    a_sem, t_sem, s_send, s_recv, p_send, p_recv, f_send, f_recv = scratch[16 + C :]
     me = lax.axis_index("str")
     pos = lax.axis_index("fac")
     fac, part = split_position(pos, F)
@@ -61,8 +61,10 @@
         )
     ]
 
+    strip = A * T // 8
+
     def load(k):
-        return pltpu.make_async_copy(amp_hbm.at[part, :, pl.ds(pl.multiple_of(k * T, T), T)], amp.at[k], a_sem.at[k])
+        return pltpu.make_async_copy(amp_hbm.at[part, pl.ds(k * strip, strip)], raw.at[pl.ds(k * strip, strip)], a_sem.at[k])
 
     def start_load(k, _):
         load(k).start()
@@ -70,12 +72,12 @@
 
     for copy in tables[:5]:
         copy.start()
-    lax.fori_loop(0, NB, start_load, 0)
+    lax.fori_loop(0, 8, start_load, 0)
     for copy in tables[5:]:
         copy.start()
 
     def signs(flips, block):
-        value = flips[:, pl.ds(pl.multiple_of(block * T, T), T)].astype(jnp.float32)
+        value = flips[:, pl.ds(block * T if isinstance(block, int) else pl.multiple_of(block * T, T), T)].astype(jnp.float32)
         mine = lax.broadcasted_iota(jnp.int32, value.shape, 0) == fac
         return 1 - 2 * jnp.sum(jnp.where(mine, value, 0.0), axis=0, keepdims=True)
 
@@ -90,12 +92,15 @@
     tables[0].wait()
     tables[3].wait()
 
-    def sign(k, _):
-        load(k).wait()
-        amp[k] = amp[k] * signs(bflip, k).astype(jnp.bfloat16) * sign_a[...]
+    def sign(r, _):
+        load(r).wait()
+        rows = pl.ds(pl.multiple_of(r * strip, strip), strip)
+        row_sign = sign_a[rows, :]
+        for k in range(NB):
+            amp[k, rows, :] = raw[rows, pl.ds(k * T, T)] * signs(bflip, k).astype(jnp.bfloat16) * row_sign
         return 0
 
-    lax.fori_loop(0, NB, sign, 0)
+    lax.fori_loop(0, 8, sign, 0)
     pl.semaphore_wait(barrier, S - 1 + chips)
 
     mid = S // 2
@@ -259,7 +264,7 @@
     total = height * S
     A = height // T
     C = width // S // T
-    assert F == 2 * NF and parts == 2 and NF % 2 == 0 and K <= NB
+    assert F == 2 * NF and parts == 2 and NF % 2 == 0 and height % 128 == 0
     per = total // F
     H = math.gcd(per // T, 4)
     ids = (beta_index.transpose(2, 0, 1), alpha_index.transpose(2, 0, 1), beta_tile, alpha_tile)
@@ -287,9 +292,10 @@
             pltpu.SMEM((K, NF, NB), jnp.int32),
             pltpu.SMEM((NF, K), jnp.int32),
             pltpu.SMEM((NF, K), jnp.int32),
+            pltpu.VMEM((height, width), bf16),
         ]
         + [pltpu.VMEM((NB, T, T), bf16) for _ in range(C)]
-        + [dma((NB,)), dma((8,)), dma((C, S)), dma((C, S))]
+        + [dma((8,)), dma((8,)), dma((C, S)), dma((C, S))]
         + [dma((C, F // 2, H)) for _ in range(4)],
         compiler_params=pltpu.CompilerParams(collective_id=0, has_side_effects=True, vmem_limit_bytes=67043328),
         name="sigma",

time: 116 us -> 116 us (level)
  no operation moved by 1% of the time
where the time goes in v4:
time: 116 us
  Pallas kernels  112 us (97%)
  other arithmetic  4.2 us (4%)
    pallas_call x1, Pallas kernels, local(): pl.pallas_call(functools.partial(kernel, (S, F, C, A, T, K, NB, H)), out_...  112 us
    reduce_sum x1, other arithmetic, local(): return jnp.sum(terms.astype(jnp.float32), axis=0)  4.2 us

profile of v4, /device:TPU:0, one launch (start us, length us, event | category | flops | bytes accessed | tf_op | source)
XLA Modules:
  0.0 115.8 jit_solution(3004181289544244895)
XLA Ops:
  0.0 111.6 %sigma.1 = bf16[1,2,1024,512]{3,2,1,0:T(8,128)(2,1)} custom-call(bf16[2,512,4096]{2,1,0:T(8,128)(2,1)} %amp_hbm.1, s32[2,4096]{1,0:T(2,128)} %bflip_hbm.1, s32[2,4096]{1,0:T(2,128)} %aflip_hbm.1, bf16[16,128,128]{2,1,0:T(8,128)(2,1)} %btab_hbm.1, bf16[16,128,128]{2,1,0:T(8,128)(2,1)} %atab_hbm.1, s32[12,2,32]{2,1,0:T(2,128)} %bitcast.5, ...), custom_call_target="tpu_custom_call" | custom-call | tf_op jit(solution)/shard_map/sigma/pallas_call | solution.py:274
  111.6 4.2 %bitcast_convert_fusion = f32[2,1024,512]{2,1,0:T(8,128)} fusion(bf16[1,2,1024,512]{3,2,1,0:T(8,128)(2,1)} %sigma.1), kind=kLoop, calls=%fused_computation | loop fusion | flops 1048576 | bytes 6291456 | tf_op jit(solution)/shard_map/reduce_sum | solution.py:303
